TPU v7x, 128 devices: a whole 4x4x4 slice. The times are simulated.
128 devices in a mesh: layer: 4 (over y_lo, core), shard: 32 (over z, y_hi, x).
Axes of the slice: x: 4, y: 4 (y_hi: 2, y_lo: 2; y = y_hi * 2 + y_lo), z: 4, core: 2. Of those that a mesh axis runs over, the one named last changes fastest.
Arguments:
- input_acts: bfloat16 [8, 16384, 5120], P('layer', 'shard'), may hold values from -6 to 6
- output_grads: bfloat16 [8, 16384, 1024], P('layer', 'shard'), may hold values from -6 to 6
- input_inverse: bfloat16 [8, 5120, 5120], P('layer', 'shard'), may hold values from -1 to 2, as said below
- output_inverse: bfloat16 [8, 1024, 1024], P('layer', 'shard'), may hold values from -1 to 2, as said below
- query_input: bfloat16 [8, 5120, 512], P(None, 'shard'), may hold values from -0.0048828125 to 0.0048828125
- query_output: bfloat16 [8, 1024, 512], P(None, 'shard'), may hold values from -0.1875 to 0.1875
- layer_order: int32 [8], replicated, may hold values from 0 to 7, each once
Outputs:
- scores: float32 [16384, 16], P('shard', 'layer')
Inputs may be any that keep to these rules, and one draw needn't show every extreme that they name: `input_inverse`: symmetric in its last two dimensions, with a unit-sized diagonal. `output_inverse`: symmetric in its last two dimensions, with a unit-sized diagonal.
All inputs are finite; a program needn't handle non-finite values.
Results may differ from a plain program's by a relative error of at most 0.0045.
Values may be sent and summed in bfloat16 or wider, within the bound.
A program may use at most 128 MiB of HBM per device.

v0:
```python
import jax
import jax.numpy as jnp
from jax import lax
from jax.sharding import PartitionSpec as P

QUERIES = 16


def joined_along(tiles, dim):
    dims = list(tiles.shape[1:])
    dims[dim] *= tiles.shape[0]
    return jnp.moveaxis(tiles, 0, dim).reshape(dims)


def sent_to_all(shard, axis):
    devices = lax.axis_size(axis)
    return lax.all_to_all(
        jnp.broadcast_to(shard[None], (devices, *shard.shape)), axis, 0, 0, tiled=True
    )


def gather_directly(shard, axis, dim):
    return joined_along(sent_to_all(shard, axis), dim)


def shards(
    input_acts, output_grads, input_inverse, output_inverse, query_input, query_output, layer_order
):
    depth = input_acts.shape[0]
    tokens = input_acts.shape[1]
    first = lax.axis_index("layer") * depth
    chosen_in = []
    chosen_out = []
    for position in range(depth):
        model_layer = layer_order[first + position]
        chosen_in.append(lax.dynamic_index_in_dim(query_input, model_layer, 0, keepdims=False))
        chosen_out.append(lax.dynamic_index_in_dim(query_output, model_layer, 0, keepdims=False))
    vectors_in = jnp.stack(chosen_in, axis=1)
    vectors_out = jnp.stack(chosen_out, axis=1)
    width = vectors_in.shape[2]
    whole_in = lax.all_gather(vectors_in, "shard", axis=0, tiled=True)
    folded_in = jnp.einsum(
        "jsk,kjn->sjn", input_inverse, whole_in, preferred_element_type=jnp.float32
    ).astype(jnp.bfloat16)
    columns = input_acts
    left = jnp.einsum(
        "jti,ijn->jtn",
        columns,
        lax.all_gather(folded_in, "shard", axis=0, tiled=True),
        preferred_element_type=jnp.float32,
    )
    whole_out = gather_directly(vectors_out, "shard", 0)
    folded_out = jnp.einsum(
        "jsk,kjn->sjn", output_inverse, whole_out, preferred_element_type=jnp.float32
    ).astype(jnp.bfloat16)
    columns = output_grads
    right = jnp.einsum(
        "jti,ijn->jtn",
        columns,
        gather_directly(folded_out, "shard", 0),
        preferred_element_type=jnp.float32,
    )
    product = (left * right).reshape(depth, tokens, QUERIES, width // QUERIES).sum(axis=(0, 3))
    return lax.psum_scatter(product, "layer", scatter_dimension=1, tiled=True)


def solution(mesh):
    in_specs = (
        P("layer", "shard", None),
        P("layer", "shard", None),
        P("layer", "shard", None),
        P("layer", "shard", None),
        P(None, "shard", None),
        P(None, "shard", None),
        P(),
    )
    out_specs = P("shard", "layer")
    return jax.shard_map(shards, mesh=mesh, in_specs=in_specs, out_specs=out_specs, check_vma=False)
```

profile of v0, /device:TPU:1, one launch (start us, length us, event | category | flops | bytes accessed | tf_op | source)
XLA Modules:
  0.0 326.5 jit_solution(4169752645969869274)
XLA Ops:
  6.5 1.4 fusion.2
  11.6 1.0 dynamic-slice_bitcast_fusion.1
  12.6 0.8 pad_maximum_fusion
  13.4 0.0 all-gather.3.cloned.1.call-update
  13.4 0.0 all-gather.5.cloned.1.call-start
  13.4 119.2 %all-gather.3.cloned.1.call-done = bf16[5120,2,512]{2,0,1:T(8,128)(2,1)} async-done(((bf16[160,2,512]{2,0,1:T(8,128)(2,1)}), bf16[5120,2,512]{2,0,1:T(8,128)(2,1)}) %all-gather.3.cloned.1.call-update) | async-done | bytes 10485776 | tf_op jit(solution)/shard_map/all_gather | solution.py:41
  132.7 6.6 %fusion = bf16[160,2,512]{2,0,1:T(8,128)(2,1)} fusion(bf16[2,160,5120]{2,1,0:T(8,128)(2,1)S(1)} %copy-done, bf16[5120,2,512]{2,0,1:T(8,128)(2,1)} %all-gather.3.cloned.1.call-done), kind=kOutput, calls=%fused_computation.2 | convolution fusion | flops 1677885440 | bytes 14090240 | tf_op jit(solution)/shard_map/jsk,kjn->sjn/dot_general | solution.py:42
  139.3 0.8 dynamic-slice_bitcast_fusion.3
  140.1 0.2 broadcast_in_dim.4
  140.3 36.1 %all_to_all.10 = bf16[32,32,2,512]{3,1,2,0:T(8,128)(2,1)S(1)} all-to-all(bf16[32,32,2,512]{3,1,2,0:T(8,128)(2,1)S(1)} %broadcast_in_dim.4), channel_id=1, replica_groups=mesh['layer'=4,'shard'=32] {'shard'}, dimensions={0} | all-to-all | bytes 4194304 | tf_op jit(solution)/shard_map/all_to_all | solution.py:17
  176.5 0.2 copy.13
  176.7 0.7 copy-done.1
  177.4 0.4 fusion.1
  177.8 1.6 broadcast_in_dim.5
  179.4 5.1 %all-to-all-start.1 = ((bf16[32,32,2,512]{3,1,2,0:T(8,128)(2,1)}), bf16[32,32,2,512]{3,1,2,0:T(8,128)(2,1)}, u32[]{:S(2)}, u32[]{:S(2)}) async-start(bf16[32,32,2,512]{3,1,2,0:T(8,128)(2,1)} %broadcast_in_dim.5), calls=%async_computation.1 | async-start | bytes 4194304 | tf_op jit(solution)/shard_map/all_to_all | solution.py:17
  184.5 0.6 dynamic-slice
  185.7 34.5 %all-to-all-done.1 = bf16[32,32,2,512]{3,1,2,0:T(8,128)(2,1)} async-done(((bf16[32,32,2,512]{3,1,2,0:T(8,128)(2,1)}), bf16[32,32,2,512]{3,1,2,0:T(8,128)(2,1)}, u32[]{:S(2)}, u32[]{:S(2)}) %all-to-all-start.1) | async-done | bytes 2097184 | tf_op jit(solution)/shard_map/all_to_all | solution.py:17
  220.2 3.2 copy.14
  223.4 66.7 %all-gather.5.cloned.1.call-done = bf16[5120,2,512]{2,0,1:T(8,128)(2,1)} async-done(((bf16[160,2,512]{2,0,1:T(8,128)(2,1)}), bf16[5120,2,512]{2,0,1:T(8,128)(2,1)}) %all-gather.5.cloned.1.call-update) | async-done | bytes 10485776 | tf_op jit(solution)/shard_map/all_gather | solution.py:49
  290.1 13.7 %fusion.3 = f32[2,512,512]{2,1,0:T(8,128)} fusion(bf16[5120,2,512]{2,0,1:T(8,128)(2,1)} %all-gather.5.cloned.1.call-done, bf16[2,512,5120]{2,1,0:T(8,128)(2,1)} %param.7), kind=kOutput, calls=%fused_computation.14 | convolution fusion | flops 5368709120 | bytes 23068672 | tf_op jit(solution)/shard_map/jti,ijn->jtn/dot_general | solution.py:46
  303.7 4.6 %multiply_reduce_fusion = f32[512,512]{1,0:T(8,128)S(1)} fusion(f32[2,512,512]{2,1,0:T(8,128)} %fusion.3, bf16[1024,2,512]{2,0,1:T(8,128)(2,1)} %bitcast.29, bf16[2,512,1024]{2,1,0:T(8,128)(2,1)} %param.8), kind=kOutput, calls=%fused_computation | convolution fusion | flops 1074528256 | bytes 7340032 | tf_op jit(solution)/shard_map/jti,ijn->jtn/dot_general | solution.py:57
  308.3 0.2 bitcast_reduce_fusion
  308.5 10.6 %all-reduce = f32[512,16]{0,1:T(8,128)S(1)} all-reduce(f32[512,16]{0,1:T(8,128)S(1)} %bitcast_reduce_fusion), channel_id=2, replica_groups=mesh['layer'=4,'shard'=32] {'layer'}, use_global_device_ids=true, to_apply=%region_2.3.clone | all-reduce | flops 8192 | bytes 65536
  319.0 0.6 constant_dynamic-slice_fusion
  (8 shorter events, 0.0 us)
Async XLA Ops:
  6.5 126.1 %copy-start = (bf16[2,160,5120]{2,1,0:T(8,128)(2,1)S(1)}, bf16[2,160,5120]{2,1,0:T(8,128)(2,1)}, u32[]{:S(2)}) copy-start(bf16[2,160,5120]{2,1,0:T(8,128)(2,1)} %param.9) | copy-start | bytes 9830404
  6.5 126.1 %all-gather.3.cloned.1.call-start = ((), (), s32[]{:S(2)}) async-start(), calls=%async_computation.2 | async-start | bytes 10813440 | tf_op jit(solution)/shard_map/all_gather | solution.py:41
  13.4 276.7 %all-gather.5.cloned.1.call-start = ((), (), s32[]{:S(2)}) async-start(), calls=%async_computation.3 | async-start | bytes 10813440 | tf_op jit(solution)/shard_map/all_gather | solution.py:49
  176.4 0.9 copy-start.1
  179.4 5.1 %copy-start.2 = (u32[128]{0:T(128)S(1)}, u32[128]{0:T(128)}, u32[]{:S(2)}) copy-start(u32[128]{0:T(128)} %constant.36) | copy-start | bytes 1540
  179.4 40.8 %all-to-all-start.1 = ((bf16[32,32,2,512]{3,1,2,0:T(8,128)(2,1)}), bf16[32,32,2,512]{3,1,2,0:T(8,128)(2,1)}, u32[]{:S(2)}, u32[]{:S(2)}) async-start(bf16[32,32,2,512]{3,1,2,0:T(8,128)(2,1)} %broadcast_in_dim.5), calls=%async_computation.1 | async-start | bytes 4194304 | tf_op jit(solution)/shard_map/all_to_all | solution.py:17
Sparse Core Ops, SparseCore 0:
  13.5 119.1 all-gather.2
  139.4 150.6 all-gather.4
where the time goes:
time: 327 us; the launch traced here: 326 us
  waiting for transfers between devices  220 us (67%)
  blocking collectives  46.7 us (14%)
  matrix products  25.3 us (8%)
  between operations  17.7 us (5%)
  local copies, waits for them, and re-layouts  10.3 us (3%)
  starting transfers between devices  5.12 us (2%)
    all_gather x1, waiting for transfers between devices, shards(): whole_in = lax.all_gather(vectors_in, 'shard', axis=0, tiled=True)  119 us
    all_gather x1, waiting for transfers between devices, shards(): lax.all_gather(folded_in, 'shard', axis=0, tiled=True)  66.7 us
    all_to_all x1, blocking collectives, sent_to_all(): lax.all_to_all(jnp.broadcast_to(shard[None], (devices, *shard.shape)), ax...  36.1 us
    all_to_all x1, waiting for transfers between devices, sent_to_all(): lax.all_to_all(jnp.broadcast_to(shard[None], (devices, *shard.shape)), ax...  34.5 us
    dot_general x1, matrix products, shards(): jnp.einsum('jti,ijn->jtn', columns, lax.all_gather(folded_in, 'shard', ax...  13.7 us
    unnamed x1, blocking collectives  10.6 us
    dot_general x1, matrix products, shards(): jnp.einsum('jsk,kjn->sjn', input_inverse, whole_in, preferred_element_typ...  6.58 us
  transfers between devices with their start and end apart: 3, of which 3 were waited for; matrix products, arithmetic and copies ran while one was open for 2% of the time, Pallas kernels for 0%

commit v1 on v0

--- a/solution.py
+++ b/solution.py
@@ -38,7 +38,10 @@
     vectors_in = jnp.stack(chosen_in, axis=1)
     vectors_out = jnp.stack(chosen_out, axis=1)
     width = vectors_in.shape[2]
-    whole_in = lax.all_gather(vectors_in, "shard", axis=0, tiled=True)
+    size = lax.axis_size("shard")
+    parts = jnp.stack([vectors_in for _ in range(size)])
+    parts = lax.all_to_all(parts, "shard", split_axis=0, concat_axis=0)
+    whole_in = jnp.concatenate(parts, axis=0)
     folded_in = jnp.einsum(
         "jsk,kjn->sjn", input_inverse, whole_in, preferred_element_type=jnp.float32
     ).astype(jnp.bfloat16)

time: 327 us -> 351 us (1.073)
  blocking collectives: 46.7 us -> 176 us
  waiting for transfers between devices: 220 us -> 103 us
  local copies, waits for them, and re-layouts: 10.3 us -> 22.9 us
    all_to_all x0 -> x1, blocking collectives: none -> 129 us  [shards(): parts = lax.all_to_all(parts, 'shard', split_axis=0, concat_axis=0)]
    all_gather x1 -> x0, waiting for transfers between devices: 119 us -> none  [shards(): whole_in = lax.all_gather(vectors_in, 'shard', axis=0, tiled=True)]
    all_to_all x0 -> x1, local copies, waits for them, and re-layouts: none -> 9.05 us  [shards(): parts = lax.all_to_all(parts, 'shard', split_axis=0, concat_axis=0)]
    another operation x0 -> x1, local copies, waits for them, and re-layouts: none -> 5.1 us  [shards(): parts = jnp.stack([vectors_in for _ in range(size)])]
  transfers between devices with their start and end apart: 3 -> 2, of which waited for: 3 -> 2; matrix products, arithmetic and copies ran while one was open for 2% -> 2% of each run, Pallas kernels for 0% -> 0%
where the time goes in v1:
time: 351 us
  blocking collectives  176 us (50%)
  waiting for transfers between devices  103 us (29%)
  matrix products  25.4 us (7%)
  local copies, waits for them, and re-layouts  22.9 us (7%)
  between operations  17.9 us (5%)
  starting transfers between devices  4.82 us (1%)
    all_to_all x1, blocking collectives, shards(): parts = lax.all_to_all(parts, 'shard', split_axis=0, concat_axis=0)  129 us
    all_gather x1, waiting for transfers between devices, shards(): lax.all_gather(folded_in, 'shard', axis=0, tiled=True)  68.4 us
    all_to_all x1, blocking collectives, sent_to_all(): lax.all_to_all(jnp.broadcast_to(shard[None], (devices, *shard.shape)), ax...  36.3 us
    all_to_all x1, waiting for transfers between devices, sent_to_all(): lax.all_to_all(jnp.broadcast_to(shard[None], (devices, *shard.shape)), ax...  34.9 us
    dot_general x1, matrix products, shards(): jnp.einsum('jti,ijn->jtn', columns, lax.all_gather(folded_in, 'shard', ax...  13.7 us
    unnamed x1, blocking collectives  10.6 us
    all_to_all x1, local copies, waits for them, and re-layouts, shards(): parts = lax.all_to_all(parts, 'shard', split_axis=0, concat_axis=0)  9.05 us
  transfers between devices with their start and end apart: 2, of which 2 were waited for; matrix products, arithmetic and copies ran while one was open for 2% of the time, Pallas kernels for 0%

profile of v1, /device:TPU:1, one launch (start us, length us, event | category | flops | bytes accessed | tf_op | source)
XLA Modules:
  0.0 350.9 jit_solution(5407998632939976864)
XLA Ops:
  6.5 1.4 fusion.2
  11.7 1.0 dynamic-slice_bitcast_fusion.1
  12.8 5.1 %stack.17 = bf16[32,160,2,512]{3,1,2,0:T(8,128)(2,1)} broadcast(bf16[160,2,512]{2,0,1:T(8,128)(2,1)S(1)} %pad_maximum_fusion), dimensions={1,2,3} | broadcast | bytes 10813440 | tf_op jit(solution)/shard_map/stack | solution.py:42
  17.9 129.5 %all_to_all.15 = bf16[32,160,2,512]{3,1,2,0:T(8,128)(2,1)} all-to-all(bf16[32,160,2,512]{3,1,2,0:T(8,128)(2,1)} %stack.17), channel_id=1, replica_groups=mesh['layer'=4,'shard'=32] {'shard'}, dimensions={0} | all-to-all | bytes 20971520 | tf_op jit(solution)/shard_map/all_to_all | solution.py:43
  147.4 9.1 %copy.18 = bf16[32,160,2,512]{3,1,0,2:T(8,128)(2,1)} copy(bf16[32,160,2,512]{3,1,2,0:T(8,128)(2,1)} %all_to_all.15) | data formatting | bytes 20971520 | tf_op jit(solution)/shard_map/all_to_all | solution.py:43
  156.5 6.6 %fusion = bf16[160,2,512]{2,0,1:T(8,128)(2,1)} fusion(bf16[2,160,5120]{2,1,0:T(8,128)(2,1)S(1)} %copy-done, bf16[5120,2,512]{2,0,1:T(8,128)(2,1)} %bitcast.30), kind=kOutput, calls=%fused_computation.2 | convolution fusion | flops 1677885440 | bytes 14090240 | tf_op jit(solution)/shard_map/jsk,kjn->sjn/dot_general | solution.py:45
  163.0 0.0 all-gather.2.cloned.1.call-update
  163.1 0.8 dynamic-slice_bitcast_fusion.3
  163.9 0.2 broadcast_in_dim.4
  164.1 36.3 %all_to_all.16 = bf16[32,32,2,512]{3,1,2,0:T(8,128)(2,1)S(1)} all-to-all(bf16[32,32,2,512]{3,1,2,0:T(8,128)(2,1)S(1)} %broadcast_in_dim.4), channel_id=1, replica_groups=mesh['layer'=4,'shard'=32] {'shard'}, dimensions={0} | all-to-all | bytes 4194304 | tf_op jit(solution)/shard_map/all_to_all | solution.py:17
  200.4 0.2 copy.19
  200.7 0.7 copy-done.2
  201.3 0.4 fusion.1
  201.8 1.6 broadcast_in_dim.5
  203.4 4.8 %all-to-all-start.2 = ((bf16[32,32,2,512]{3,1,2,0:T(8,128)(2,1)}), bf16[32,32,2,512]{3,1,2,0:T(8,128)(2,1)S(1)}, u32[]{:S(2)}, u32[]{:S(2)}) async-start(bf16[32,32,2,512]{3,1,2,0:T(8,128)(2,1)} %broadcast_in_dim.5), calls=%async_computation.2 | async-start | bytes 4194304 | tf_op jit(solution)/shard_map/all_to_all | solution.py:17
  208.2 0.6 dynamic-slice
  209.4 34.9 %all-to-all-done.2 = bf16[32,32,2,512]{3,1,2,0:T(8,128)(2,1)S(1)} async-done(((bf16[32,32,2,512]{3,1,2,0:T(8,128)(2,1)}), bf16[32,32,2,512]{3,1,2,0:T(8,128)(2,1)S(1)}, u32[]{:S(2)}, u32[]{:S(2)}) %all-to-all-start.2) | async-done | bytes 2097184 | tf_op jit(solution)/shard_map/all_to_all | solution.py:17
  244.4 1.6 copy.20
  245.9 68.4 %all-gather.2.cloned.1.call-done = bf16[5120,2,512]{2,0,1:T(8,128)(2,1)} async-done(((bf16[160,2,512]{2,0,1:T(8,128)(2,1)}), bf16[5120,2,512]{2,0,1:T(8,128)(2,1)}) %all-gather.2.cloned.1.call-update) | async-done | bytes 10485776 | tf_op jit(solution)/shard_map/all_gather | solution.py:52
  314.3 13.7 %fusion.3 = f32[2,512,512]{2,1,0:T(8,128)} fusion(bf16[5120,2,512]{2,0,1:T(8,128)(2,1)} %all-gather.2.cloned.1.call-done, bf16[2,512,5120]{2,1,0:T(8,128)(2,1)} %param.7), kind=kOutput, calls=%fused_computation.14 | convolution fusion | flops 5368709120 | bytes 23068672 | tf_op jit(solution)/shard_map/jti,ijn->jtn/dot_general | solution.py:49
  328.0 4.7 %multiply_reduce_fusion = f32[512,512]{1,0:T(8,128)S(1)} fusion(f32[2,512,512]{2,1,0:T(8,128)} %fusion.3, bf16[1024,2,512]{2,0,1:T(8,128)(2,1)} %bitcast.31, bf16[2,512,1024]{2,1,0:T(8,128)(2,1)} %param.8), kind=kOutput, calls=%fused_computation | convolution fusion | flops 1074528256 | bytes 7340032 | tf_op jit(solution)/shard_map/jti,ijn->jtn/dot_general | solution.py:60
  332.7 0.2 bitcast_reduce_fusion
  332.9 10.6 %all-reduce = f32[512,16]{0,1:T(8,128)S(1)} all-reduce(f32[512,16]{0,1:T(8,128)S(1)} %bitcast_reduce_fusion), channel_id=2, replica_groups=mesh['layer'=4,'shard'=32] {'layer'}, use_global_device_ids=true, to_apply=%region_2.3.clone | all-reduce | flops 8192 | bytes 65536
  343.4 0.6 constant_dynamic-slice_fusion
  (10 shorter events, 0.1 us)
Async XLA Ops:
  6.5 149.9 %copy-start = (bf16[2,160,5120]{2,1,0:T(8,128)(2,1)S(1)}, bf16[2,160,5120]{2,1,0:T(8,128)(2,1)}, u32[]{:S(2)}) copy-start(bf16[2,160,5120]{2,1,0:T(8,128)(2,1)} %param.9) | copy-start | bytes 9830404
  6.5 307.8 %all-gather.2.cloned.1.call-start = ((), (), s32[]{:S(2)}) async-start(), calls=%async_computation.3 | async-start | bytes 10813440 | tf_op jit(solution)/shard_map/all_gather | solution.py:52
  200.4 0.9 copy-start.2
  203.4 4.8 %copy-start.3 = (u32[128]{0:T(128)S(1)}, u32[128]{0:T(128)}, u32[]{:S(2)}) copy-start(u32[128]{0:T(128)} %constant.36) | copy-start | bytes 1540
  203.4 41.0 %all-to-all-start.2 = ((bf16[32,32,2,512]{3,1,2,0:T(8,128)(2,1)}), bf16[32,32,2,512]{3,1,2,0:T(8,128)(2,1)S(1)}, u32[]{:S(2)}, u32[]{:S(2)}) async-start(bf16[32,32,2,512]{3,1,2,0:T(8,128)(2,1)} %broadcast_in_dim.5), calls=%async_computation.2 | async-start | bytes 4194304 | tf_op jit(solution)/shard_map/all_to_all | solution.py:17
  328.0 16.1 %copy-start.1 = (bf16[2,160,5120]{2,1,0:T(8,128)(2,1)S(1)}, bf16[2,160,5120]{2,1,0:T(8,128)(2,1)}, u32[]{:S(2)}) copy-start(bf16[2,160,5120]{2,1,0:T(8,128)(2,1)} %param.9) | copy-start | bytes 9830404
Sparse Core Ops, SparseCore 0:
  163.2 151.0 all-gather.1
